TPU v7x, 32 devices: a whole 2x2x4 slice. The times are simulated.
32 devices in a mesh: seg: 2 (over x), ch: 16 (over z, y, core).
Axes of the slice: x: 2, y: 2, z: 4, core: 2. Of those that a mesh axis runs over, the one named last changes fastest.
Arguments:
- recording: bfloat16 [1024, 4096], P('ch', 'seg'), parts along dimension 1, may hold values from -300 to 300
- live_mask: int32 [4096], P('seg'), parts along dimension 0, may hold values 0 or 1
- window_starts: int32 [64], P('seg'), parts along dimension 0, may hold values from 0 to 512, as said below
- source_order: int32 [4], P('seg'), parts along dimension 0, may hold values from 0 to 15
Outputs:
- correlations: bfloat16 [2, 128, 4096, 128], P(None, None, ('seg', 'ch')), parts along dimension 2
There are 2 independent parts, one for each index of `seg`. A program takes and returns all parts, laid end to end along the dimension named above; each array names one. Nothing has to cross between parts.
Inputs may be any that keep to these rules, and one draw needn't show every extreme that they name: `window_starts`: the first start is 0 and the last is 512; the others are in no order and may repeat. `source_order`: block b is the channels b * 128 to (b + 1) * 128 - 1; blocks may repeat.
All inputs are finite; a program needn't handle non-finite values.
Results may differ from a plain program's by a relative error of at most 0.0059.
Values may be sent and summed in bfloat16 or wider, within the bound.
No kernel may reach another device: no remote copies, remote signals or barrier semaphores. Data moves between devices by JAX's collectives and lax.ppermute only.
A program may use at most 128 MiB of HBM per device.

v0:
```python
import math
import jax
import jax.numpy as jnp
from jax import lax
from jax.sharding import PartitionSpec as P

CH_DEV = 128
WIN = 512
NF = 128
F0 = 4
LAGS = 128
HALF = 64
BAND = 64
K = 2
NWIN = 32
STABILIZER_FLOOR = 1e-06


def broadcast(value, axis, source):
    kept = jnp.where(lax.axis_index(axis) == source, value, 0).astype(value.dtype)
    return lax.psum(kept, axis)


def banded(length, radius, number_type):
    row_index = jnp.arange(length)[:, None]
    col_index = jnp.arange(length)[None, :]
    return (jnp.abs(row_index - col_index) <= radius).astype(number_type)


def forward_table():
    phases = jnp.arange(WIN)[:, None] * (F0 + jnp.arange(NF))[None, :] % WIN
    angles = phases.astype(jnp.float32) * (2.0 * math.pi / WIN)
    return jnp.stack([jnp.cos(angles), -jnp.sin(angles)], axis=1).astype(jnp.bfloat16)


def inverse_table():
    phases = (F0 + jnp.arange(NF))[:, None] * (jnp.arange(LAGS)[None, :] - LAGS // 2) % WIN
    angles = phases.astype(jnp.float32) * (2.0 * math.pi / WIN)
    return jnp.stack([jnp.cos(angles), -jnp.sin(angles)], axis=0).astype(jnp.bfloat16)


def whiten(columns, window_starts, mask_portion):
    windows = jax.vmap(lambda start_shift: lax.dynamic_slice_in_dim(columns, start_shift, WIN, 0))(
        window_starts
    )
    values = windows.astype(jnp.float32)
    centred = values - jnp.mean(values, axis=1, keepdims=True)
    magnitude = jnp.abs(centred).astype(jnp.bfloat16)
    time_band = banded(WIN, HALF, jnp.bfloat16)
    time_counts = jnp.sum(time_band.astype(jnp.float32), axis=1)
    running = (
        jnp.einsum("jk,wkc->wjc", time_band, magnitude, preferred_element_type=jnp.float32)
        / time_counts[None, :, None]
    )
    normalized = (centred / (running + STABILIZER_FLOOR)).astype(jnp.bfloat16)
    channel_spectra = jnp.einsum(
        "wjc,jrf->wrfc", normalized, forward_table(), preferred_element_type=jnp.float32
    )
    amplitude = jnp.sqrt(
        channel_spectra[:, 0] * channel_spectra[:, 0]
        + channel_spectra[:, 1] * channel_spectra[:, 1]
    )
    bin_band = banded(NF, BAND, jnp.float32)
    smoothed_spectrum = (
        jnp.einsum("fg,wgc->wfc", bin_band, amplitude, precision=lax.Precision.HIGHEST)
        / jnp.sum(bin_band, axis=1)[None, :, None]
    )
    channel_alive_flags = mask_portion.astype(jnp.float32)
    return (
        channel_spectra / (smoothed_spectrum[:, None] + STABILIZER_FLOOR) * channel_alive_flags
    ).astype(jnp.bfloat16)


def stack_block(source, receivers, inverse):
    product = jnp.einsum("wrfs,wrfc->fsc", source, receivers, preferred_element_type=jnp.float32)
    cross_spec = (product / NWIN).astype(jnp.bfloat16)
    matched_pairs = cross_spec.reshape(NF, cross_spec.shape[1], 2, cross_spec.shape[2] // 2)
    lagged = jnp.einsum("fsrc,rft->sct", matched_pairs, inverse, preferred_element_type=jnp.float32)
    return (lagged * math.sqrt(NWIN / NF)).astype(jnp.bfloat16)


def local(recording, live_mask, window_starts, source_order):
    block_width = CH_DEV
    regrouped = lax.all_to_all(recording, "ch", split_axis=1, concat_axis=0, tiled=True)
    own_mask = lax.dynamic_slice_in_dim(
        live_mask, lax.axis_index("ch") * block_width, block_width, 0
    )
    whitened = whiten(regrouped, window_starts, own_mask)
    swapped = jnp.stack([whitened[:, 1], -whitened[:, 0]], axis=1)
    receivers = jnp.concatenate([whitened, swapped], axis=3)
    inverse = inverse_table()
    results = []
    for number in range(K):
        source = broadcast(whitened, "ch", source_order[number])
        results.append(stack_block(source, receivers, inverse))
    return jnp.stack(results)


def solution(mesh):
    in_specs = (P("ch", "seg"), P("seg"), P("seg"), P("seg"))
    out_specs = P(None, None, ("seg", "ch"), None)
    return jax.shard_map(local, mesh=mesh, in_specs=in_specs, out_specs=out_specs, check_vma=False)
```

profile of v0, /device:TPU:0, one launch (start us, length us, event | category | flops | bytes accessed | tf_op | source)
XLA Modules:
  0.0 295.2 jit_solution(15699077252839965585)
XLA Ops:
  8.3 7.4 %all-to-all-start = ((bf16[64,16,128]{2,0,1:T(8,128)(2,1)}), bf16[64,16,128]{2,0,1:T(8,128)(2,1)S(1)}, u32[]{:S(2)}, u32[]{:S(2)}) async-start(bf16[64,16,128]{2,0,1:T(8,128)(2,1)} %copy_bitcast_fusion), calls=%async_computation | async-start | bytes 524288 | tf_op jit(solution)/shard_map/all_to_all | solution.py:84
  21.2 4.5 %all-to-all-done = bf16[64,16,128]{2,0,1:T(8,128)(2,1)S(1)} async-done(((bf16[64,16,128]{2,0,1:T(8,128)(2,1)}), bf16[64,16,128]{2,0,1:T(8,128)(2,1)S(1)}, u32[]{:S(2)}, u32[]{:S(2)}) %all-to-all-start) | async-done | bytes 262176 | tf_op jit(solution)/shard_map/all_to_all | solution.py:84
  25.7 65.7 %while.1 = (s32[]{:T(128)}, bf16[1024,128]{1,0:T(8,128)(2,1)S(1)}, s32[32,2]{0,1:T(2,128)S(1)}, bf16[32,512,128]{2,1,0:T(8,128)(2,1)}, s32[]{:T(128)}) while((s32[]{:T(128)}, bf16[1024,128]{1,0:T(8,128)(2,1)S(1)}, s32[32,2]{0,1:T(2,128)S(1)}, bf16[32,512,128]{2,1,0:T(8,128)(2,1)}, s32[]{:T(128)}) %tuple.28), condition=%wide.while_cond, body=%wide.while_body.sunk | while | flops 2 | bytes 263257 | solution.py:43
  30.5 1.4 bitcast_dynamic-update-slice_fusion.2
  32.5 1.4 bitcast_dynamic-update-slice_fusion.2
  34.6 1.4 bitcast_dynamic-update-slice_fusion.2
  36.6 1.4 bitcast_dynamic-update-slice_fusion.2
  91.4 2.8 convert_reduce_fusion
  94.3 10.4 %fusion.16 = f32[32,2,128,128]{2,3,0,1:T(8,128)} fusion(f32[512]{0:T(512)S(1)} %convert_reduce_fusion.1, f32[32,128]{1,0:T(8,128)S(1)} %broadcast_multiply_fusion, bf16[32,512,128]{2,1,0:T(8,128)(2,1)} %get-tuple-element.12, bf16[512,1,128]{2,0,1:T(8,128)(2,1)S(1)} %get-tuple-element.32, bf16[512,1,128]{2,0,1:T(8,128)(2,1)S(1)} %get-tuple-element.31), kind=kOutput, calls=%fused_computation.25 | convolution fusion | flops 3243507712 | bytes 8669184 | tf_op jit(solution)/shard_map/wjc,jrf->wrfc/dot_general | solution.py:56
  104.6 4.1 %add_bitcast_fusion = f32[32,128,128]{1,2,0:T(8,128)S(1)} fusion(f32[32,2,128,128]{2,3,0,1:T(8,128)} %fusion.16, f32[128]{0:T(128)S(1)} %convert_reduce_fusion.2), kind=kOutput, calls=%fused_computation.32 | convolution fusion | flops 807976960 | bytes 6291968 | tf_op jit(solution)/shard_map/fg,wgc->wfc/dot_general | solution.py:65
  108.7 2.6 broadcast_select_fusion.1
  111.4 1.5 broadcast_select_fusion
  113.4 2.4 maximum_maximum_fusion
  115.8 8.1 %copy.16 = bf16[32,2,128,256]{3,0,1,2:T(8,128)(2,1)} copy(bf16[32,2,128,256]{2,3,0,1:T(8,128)(2,1)} %maximum_maximum_fusion) | data formatting | bytes 8388608 | tf_op jit(solution)/shard_map/concatenate | solution.py:90
  123.9 98.4 %all-reduce.4.cloned.1.call-done = (bf16[32,2,128,128]{2,3,0,1:T(8,128)(2,1)}, bf16[32,2,128,128]{2,3,0,1:T(8,128)(2,1)}) async-done(((bf16[32,2,128,128]{2,3,0,1:T(8,128)(2,1)}, bf16[32,2,128,128]{2,3,0,1:T(8,128)(2,1)}), (bf16[32,2,128,128]{2,3,0,1:T(8,128)(2,1)}, bf16[32,2,128,128]{2,3,0,1:T(8,128)(2,1)})) %all-reduce.4.cloned.1.call-update) | async-done | bytes 4194320 | tf_op jit(solution)/shard_map/psum | solution.py:21
  222.4 3.7 %copy.15 = bf16[32,2,128,128]{3,0,1,2:T(8,128)(2,1)S(1)} copy(bf16[32,2,128,128]{2,3,0,1:T(8,128)(2,1)} %get-tuple-element.22) | data formatting | bytes 4194304 | tf_op jit(solution)/shard_map/psum | solution.py:21
  226.0 8.0 %fusion.1 = bf16[128,128,256]{2,1,0:T(8,128)(2,1)} fusion(bf16[32,2,128,128]{3,0,1,2:T(8,128)(2,1)S(1)} %copy.15, bf16[32,2,128,256]{3,0,1,2:T(8,128)(2,1)} %copy.16), kind=kOutput, calls=%fused_computation.5 | convolution fusion | flops 545259520 | bytes 14680064 | tf_op jit(solution)/shard_map/wrfs,wrfc->fsc/dot_general | solution.py:75
  234.0 13.1 %copy.28 = bf16[128,128,256]{0,2,1:T(8,128)(2,1)} copy(bf16[128,128,256]{2,1,0:T(8,128)(2,1)} %fusion.1) | data formatting | bytes 16777216 | tf_op jit(solution)/shard_map/reshape | solution.py:77
  247.1 3.5 %copy.18 = bf16[32,2,128,128]{3,0,1,2:T(8,128)(2,1)S(1)} copy(bf16[32,2,128,128]{2,3,0,1:T(8,128)(2,1)} %get-tuple-element.21) | data formatting | bytes 4194304 | tf_op jit(solution)/shard_map/psum | solution.py:21
  250.6 8.0 %fusion = bf16[128,128,256]{2,1,0:T(8,128)(2,1)} fusion(bf16[32,2,128,128]{3,0,1,2:T(8,128)(2,1)S(1)} %copy.18, bf16[32,2,128,256]{3,0,1,2:T(8,128)(2,1)} %copy.16), kind=kOutput, calls=%fused_computation.3 | convolution fusion | flops 545259520 | bytes 14680064 | tf_op jit(solution)/shard_map/wrfs,wrfc->fsc/dot_general | solution.py:75
  258.6 13.1 %copy.29 = bf16[128,128,256]{0,2,1:T(8,128)(2,1)} copy(bf16[128,128,256]{2,1,0:T(8,128)(2,1)} %fusion) | data formatting | bytes 16777216 | tf_op jit(solution)/shard_map/reshape | solution.py:77
  271.7 5.9 %fusion.8 = bf16[1,128,128,128]{3,2,1,0:T(8,128)(2,1)S(1)} fusion(bf16[128,128,2,128]{0,3,2,1:T(8,128)(2,1)} %bitcast.92, bf16[1,128,128]{2,1,0:T(8,128)(2,1)S(1)} %get-tuple-element.28, bf16[1,128,128]{2,1,0:T(8,128)(2,1)S(1)} %get-tuple-element.27), kind=kOutput, calls=%fused_computation.17 | convolution fusion | flops 1077968896 | bytes 12648448 | tf_op jit(solution)/shard_map/fsrc,rft->sct/dot_general | solution.py:78
  277.6 4.3 %fusion.9 = bf16[1,128,128,128]{3,2,1,0:T(8,128)(2,1)} fusion(bf16[128,128,2,128]{0,3,2,1:T(8,128)(2,1)S(1)} %bitcast.93, bf16[1,128,128]{2,1,0:T(8,128)(2,1)S(1)} %get-tuple-element.28, bf16[1,128,128]{2,1,0:T(8,128)(2,1)S(1)} %get-tuple-element.27), kind=kOutput, calls=%fused_computation.18 | convolution fusion | flops 1077968896 | bytes 12648448 | tf_op jit(solution)/shard_map/fsrc,rft->sct/dot_general | solution.py:78
  281.9 6.4 %pad_maximum_fusion = bf16[2,128,128,128]{3,2,1,0:T(8,128)(2,1)} fusion(bf16[1,128,128,128]{3,2,1,0:T(8,128)(2,1)} %fusion.9, bf16[1,128,128,128]{3,2,1,0:T(8,128)(2,1)S(1)} %fusion.8), kind=kLoop, calls=%fused_computation.12 | loop fusion | flops 4194304 | bytes 16777216 | tf_op jit(solution)/shard_map/stack | solution.py:96
  (115 shorter events, 66.7 us)
Async XLA Ops:
  6.5 1.0 copy-start
  8.3 17.4 %all-to-all-start = ((bf16[64,16,128]{2,0,1:T(8,128)(2,1)}), bf16[64,16,128]{2,0,1:T(8,128)(2,1)S(1)}, u32[]{:S(2)}, u32[]{:S(2)}) async-start(bf16[64,16,128]{2,0,1:T(8,128)(2,1)} %copy_bitcast_fusion), calls=%async_computation | async-start | bytes 524288 | tf_op jit(solution)/shard_map/all_to_all | solution.py:84
  15.7 206.7 %all-reduce.4.cloned.1.call-start = ((), (), s32[]{:S(2)}) async-start(), calls=%async_computation.1 | async-start | bytes 8388608 | tf_op jit(solution)/shard_map/psum | solution.py:21
  104.6 4.1 %copy-start.3 = (f32[32,2,128,128]{2,3,0,1:T(8,128)S(1)}, f32[32,2,128,128]{2,3,0,1:T(8,128)}, u32[]{:S(2)}) copy-start(f32[32,2,128,128]{2,3,0,1:T(8,128)} %fusion.16) | copy-start | bytes 12582916
  271.7 5.9 %copy-start.2 = (bf16[128,128,256]{0,2,1:T(8,128)(2,1)S(1)}, bf16[128,128,256]{0,2,1:T(8,128)(2,1)}, u32[]{:S(2)}) copy-start(bf16[128,128,256]{0,2,1:T(8,128)(2,1)} %copy.29) | copy-start | bytes 25165828
  281.9 6.4 %copy-start.1 = (bf16[64,2048]{1,0:T(8,128)(2,1)S(1)}, bf16[64,2048]{1,0:T(8,128)(2,1)}, u32[]{:S(2)}) copy-start(bf16[64,2048]{1,0:T(8,128)(2,1)} %param.4) | copy-start | bytes 786436
Sparse Core Ops, SparseCore 0:
  113.0 109.3 all-reduce.3
where the time goes:
time: 297 us; the launch traced here: 295 us
  local copies, waits for them, and re-layouts  110 us (37%)
  waiting for transfers between devices  103 us (35%)
  matrix products  40.6 us (14%)
  other arithmetic  19.1 us (6%)
  between operations  14.8 us (5%)
  starting transfers between devices  7.45 us (3%)
    psum x1, waiting for transfers between devices, broadcast(): return lax.psum(kept, axis)  98.4 us
    gather x96, local copies, waits for them, and re-layouts  65.7 us
    reshape x2, local copies, waits for them, and re-layouts, stack_block(): cross_spec.reshape(NF, cross_spec.shape[1], 2, cross_spec.shape[2] // 2)  26.2 us
    dot_general x2, matrix products, stack_block(): jnp.einsum('wrfs,wrfc->fsc', source, receivers, preferred_element_type=jn...  15.9 us
    dot_general x1, matrix products, whiten(): jnp.einsum('wjc,jrf->wrfc', normalized, forward_table(), preferred_elemen...  10.4 us
    dot_general x2, matrix products, stack_block(): jnp.einsum('fsrc,rft->sct', matched_pairs, inverse, preferred_element_typ...  10.2 us
    concatenate x1, local copies, waits for them, and re-layouts, local(): receivers = jnp.concatenate([whitened, swapped], axis=3)  8.11 us
    all_to_all x1, starting transfers between devices, local(): lax.all_to_all(recording, 'ch', split_axis=1, concat_axis=0, tiled=True)  7.41 us
  transfers between devices with their start and end apart: 2, of which 2 were waited for; matrix products, arithmetic and copies ran while one was open for 5% of the time, Pallas kernels for 0%

commit v1 on v0

--- a/solution.py
+++ b/solution.py
@@ -18,7 +18,7 @@
 
 def broadcast(value, axis, source):
     kept = jnp.where(lax.axis_index(axis) == source, value, 0).astype(value.dtype)
-    return lax.psum(kept, axis)
+    return jnp.sum(lax.all_gather(kept, axis), axis=0)
 
 
 def banded(length, radius, number_type):

time: 297 us -> 530 us (1.78)
  waiting for transfers between devices: 103 us -> 310 us
  other arithmetic: 19.1 us -> 46.6 us
    all_gather x0 -> x2, waiting for transfers between devices: none -> 305 us  [broadcast(): return jnp.sum(lax.all_gather(kept, axis), axis=0)]
    psum x1 -> x0, waiting for transfers between devices: 98.4 us -> none  [broadcast(): return lax.psum(kept, axis)]
    reduce_sum x0 -> x2, other arithmetic: none -> 27.4 us  [broadcast(): return jnp.sum(lax.all_gather(kept, axis), axis=0)]
    reduce_sum x0 -> x2, local copies, waits for them, and re-layouts: none -> 8.09 us  [broadcast(): return jnp.sum(lax.all_gather(kept, axis), axis=0)]
    psum x2 -> x0, local copies, waits for them, and re-layouts: 7.17 us -> none  [broadcast(): return lax.psum(kept, axis)]
    gather x96 -> x160, local copies, waits for them, and re-layouts: 65.7 us -> 65.2 us
  transfers between devices with their start and end apart: 2 -> 3, of which waited for: 2 -> 3; matrix products, arithmetic and copies ran while one was open for 5% -> 7% of each run, Pallas kernels for 0% -> 0%
where the time goes in v1:
time: 530 us; the launch traced here: 529 us
  waiting for transfers between devices  310 us (58%)
  local copies, waits for them, and re-layouts  110 us (21%)
  other arithmetic  46.6 us (9%)
  matrix products  39 us (7%)
  between operations  14.8 us (3%)
  starting transfers between devices  7.68 us (1%)
    all_gather x2, waiting for transfers between devices, broadcast(): return jnp.sum(lax.all_gather(kept, axis), axis=0)  305 us
    gather x160, local copies, waits for them, and re-layouts  65.2 us
    reduce_sum x2, other arithmetic, broadcast(): return jnp.sum(lax.all_gather(kept, axis), axis=0)  27.4 us
    reshape x2, local copies, waits for them, and re-layouts, stack_block(): cross_spec.reshape(NF, cross_spec.shape[1], 2, cross_spec.shape[2] // 2)  25.8 us
    dot_general x2, matrix products, stack_block(): jnp.einsum('wrfs,wrfc->fsc', source, receivers, preferred_element_type=jn...  16.6 us
  transfers between devices with their start and end apart: 3, of which 3 were waited for; matrix products, arithmetic and copies ran while one was open for 7% of the time, Pallas kernels for 0%

profile of v1, /device:TPU:0, one launch (start us, length us, event | category | flops | bytes accessed | tf_op | source)
XLA Modules:
  0.0 528.6 jit_solution(5105508844299441457)
XLA Ops:
  8.2 7.4 %all-to-all-start = ((bf16[64,16,128]{2,0,1:T(8,128)(2,1)}), bf16[64,16,128]{2,0,1:T(8,128)(2,1)S(1)}, u32[]{:S(2)}, u32[]{:S(2)}) async-start(bf16[64,16,128]{2,0,1:T(8,128)(2,1)} %copy_bitcast_fusion), calls=%async_computation | async-start | bytes 524288 | tf_op jit(solution)/shard_map/all_to_all | solution.py:84
  16.4 1.3 fusion.57
  20.5 5.1 all-to-all-done
  25.7 65.7 %while.1 = (s32[]{:T(128)}, bf16[1024,128]{1,0:T(8,128)(2,1)S(1)}, s32[32,2]{0,1:T(2,128)S(1)}, bf16[32,512,128]{1,2,0:T(8,128)(2,1)}, s32[]{:T(128)}) while((s32[]{:T(128)}, bf16[1024,128]{1,0:T(8,128)(2,1)S(1)}, s32[32,2]{0,1:T(2,128)S(1)}, bf16[32,512,128]{1,2,0:T(8,128)(2,1)}, s32[]{:T(128)}) %tuple.29), condition=%wide.while_cond, body=%wide.while_body.sunk | while | flops 2 | bytes 786537 | solution.py:43
  91.4 2.8 convert_reduce_fusion
  94.2 8.2 %fusion.16 = f32[32,2,128,128]{2,3,0,1:T(8,128)} fusion(f32[512]{0:T(512)S(1)} %convert_reduce_fusion.1, f32[32,128]{1,0:T(8,128)S(1)} %broadcast_multiply_fusion, bf16[32,512,128]{1,2,0:T(8,128)(2,1)} %get-tuple-element.12, bf16[512,1,128]{2,0,1:T(8,128)(2,1)S(1)} %get-tuple-element.30, bf16[512,1,128]{2,0,1:T(8,128)(2,1)S(1)} %get-tuple-element.29), kind=kOutput, calls=%fused_computation.26 | convolution fusion | flops 3243507712 | bytes 8669184 | tf_op jit(solution)/shard_map/wjc,jrf->wrfc/dot_general | solution.py:56
  102.4 4.1 add_bitcast_fusion
  106.5 2.7 broadcast_select_fusion.1
  110.1 1.5 broadcast_select_fusion
  112.1 2.5 maximum_maximum_fusion
  114.6 8.1 %copy.22 = bf16[32,2,128,256]{3,0,1,2:T(8,128)(2,1)} copy(bf16[32,2,128,256]{2,3,0,1:T(8,128)(2,1)} %maximum_maximum_fusion) | data formatting | bytes 8388608 | tf_op jit(solution)/shard_map/concatenate | solution.py:90
  122.7 152.9 %all-gather.5.cloned.1.call-done = bf16[512,2,128,128]{2,3,0,1:T(8,128)(2,1)} async-done(((bf16[32,2,128,128]{2,3,0,1:T(8,128)(2,1)}), bf16[512,2,128,128]{2,3,0,1:T(8,128)(2,1)}) %all-gather.5.cloned.1.call-update) | async-done | bytes 33554448 | tf_op jit(solution)/shard_map/all_gather | solution.py:21
  275.6 14.4 %reduce_sum.54 = bf16[32,2,128,128]{2,3,0,1:T(8,128)(2,1)} reduce(bf16[16,32,2,128,128]{3,4,1,0,2:T(8,128)(2,1)} %bitcast.94, bf16[]{:T(256)} %constant.61.clone.1), dimensions={0}, to_apply=%region_3.4 | reduce | flops 15728640 | bytes 35651584 | tf_op jit(solution)/shard_map/reduce_sum | solution.py:21
  289.9 3.5 copy.21
  293.4 151.7 %all-gather.7.cloned.1.call-done = bf16[512,2,128,128]{2,3,0,1:T(8,128)(2,1)} async-done(((bf16[32,2,128,128]{2,3,0,1:T(8,128)(2,1)}), bf16[512,2,128,128]{2,3,0,1:T(8,128)(2,1)}) %all-gather.7.cloned.1.call-update) | async-done | bytes 33554448 | tf_op jit(solution)/shard_map/all_gather | solution.py:21
  445.2 13.1 %reduce_sum.55 = bf16[32,2,128,128]{2,3,0,1:T(8,128)(2,1)} reduce(bf16[16,32,2,128,128]{3,4,1,0,2:T(8,128)(2,1)} %bitcast.95, bf16[]{:T(256)} %constant.61.clone.1), dimensions={0}, to_apply=%region_4.5 | reduce | flops 15728640 | bytes 35651584 | tf_op jit(solution)/shard_map/reduce_sum | solution.py:21
  458.2 4.6 copy.24
  462.8 8.6 %fusion = bf16[128,128,256]{2,1,0:T(8,128)(2,1)} fusion(bf16[32,2,128,128]{3,0,1,2:T(8,128)(2,1)} %copy.24, bf16[32,2,128,256]{3,0,1,2:T(8,128)(2,1)} %copy.22), kind=kOutput, calls=%fused_computation.4 | convolution fusion | flops 545259520 | bytes 14680064 | tf_op jit(solution)/shard_map/wrfs,wrfc->fsc/dot_general | solution.py:75
  471.4 13.1 %copy.33 = bf16[128,128,256]{0,2,1:T(8,128)(2,1)} copy(bf16[128,128,256]{2,1,0:T(8,128)(2,1)} %fusion) | data formatting | bytes 16777216 | tf_op jit(solution)/shard_map/reshape | solution.py:77
  484.5 8.0 %fusion.1 = bf16[128,128,256]{2,1,0:T(8,128)(2,1)} fusion(bf16[32,2,128,128]{3,0,1,2:T(8,128)(2,1)S(1)} %copy.21, bf16[32,2,128,256]{3,0,1,2:T(8,128)(2,1)} %copy.22), kind=kOutput, calls=%fused_computation.6 | convolution fusion | flops 545259520 | bytes 14680064 | tf_op jit(solution)/shard_map/wrfs,wrfc->fsc/dot_general | solution.py:75
  492.5 12.7 %copy.32 = bf16[128,128,256]{0,2,1:T(8,128)(2,1)} copy(bf16[128,128,256]{2,1,0:T(8,128)(2,1)} %fusion.1) | data formatting | bytes 16777216 | tf_op jit(solution)/shard_map/reshape | solution.py:77
  505.2 5.9 %fusion.9 = bf16[1,128,128,128]{3,2,1,0:T(8,128)(2,1)S(1)} fusion(bf16[128,128,2,128]{0,3,2,1:T(8,128)(2,1)} %bitcast.96, bf16[1,128,128]{2,1,0:T(8,128)(2,1)S(1)} %get-tuple-element.26, bf16[1,128,128]{2,1,0:T(8,128)(2,1)S(1)} %get-tuple-element.25), kind=kOutput, calls=%fused_computation.19 | convolution fusion | flops 1077968896 | bytes 12648448 | tf_op jit(solution)/shard_map/fsrc,rft->sct/dot_general | solution.py:78
  511.1 4.3 fusion.8
  515.4 6.4 %pad_maximum_fusion = bf16[2,128,128,128]{3,2,1,0:T(8,128)(2,1)} fusion(bf16[1,128,128,128]{3,2,1,0:T(8,128)(2,1)S(1)} %fusion.9, bf16[1,128,128,128]{3,2,1,0:T(8,128)(2,1)} %fusion.8), kind=kLoop, calls=%fused_computation.13 | loop fusion | flops 4194304 | bytes 16777216 | tf_op jit(solution)/shard_map/stack | solution.py:96
  (184 shorter events, 70.6 us)
Async XLA Ops:
  6.5 1.0 copy-start
  8.2 17.4 %all-to-all-start = ((bf16[64,16,128]{2,0,1:T(8,128)(2,1)}), bf16[64,16,128]{2,0,1:T(8,128)(2,1)S(1)}, u32[]{:S(2)}, u32[]{:S(2)}) async-start(bf16[64,16,128]{2,0,1:T(8,128)(2,1)} %copy_bitcast_fusion), calls=%async_computation | async-start | bytes 524288 | tf_op jit(solution)/shard_map/all_to_all | solution.py:84
  15.7 259.9 %all-gather.5.cloned.1.call-start = ((), (), s32[]{:S(2)}) async-start(), calls=%async_computation.1 | async-start | bytes 35651584 | tf_op jit(solution)/shard_map/all_gather | solution.py:21
  102.4 4.1 copy-start.3
  109.2 336.0 %all-gather.7.cloned.1.call-start = ((), (), s32[]{:S(2)}) async-start(), calls=%async_computation.2 | async-start | bytes 35651584 | tf_op jit(solution)/shard_map/all_gather | solution.py:21
  505.2 5.9 %copy-start.2 = (bf16[128,128,256]{0,2,1:T(8,128)(2,1)S(1)}, bf16[128,128,256]{0,2,1:T(8,128)(2,1)}, u32[]{:S(2)}) copy-start(bf16[128,128,256]{0,2,1:T(8,128)(2,1)} %copy.32) | copy-start | bytes 25165828
  515.4 6.4 %copy-start.1 = (bf16[64,2048]{1,0:T(8,128)(2,1)S(1)}, bf16[64,2048]{1,0:T(8,128)(2,1)}, u32[]{:S(2)}) copy-start(bf16[64,2048]{1,0:T(8,128)(2,1)} %param.4) | copy-start | bytes 786436
Sparse Core Ops, SparseCore 0:
  109.3 166.2 all-gather.4
  277.1 168.0 all-gather.6
